TPU v7x, 32 devices: a whole 2x2x4 slice. The times are simulated.
32 devices in a mesh: kv: 2 (over x), seq: 16 (over z, y, core).
Axes of the slice: x: 2, y: 2, z: 4, core: 2. Of those that a mesh axis runs over, the one named last changes fastest.
Arguments:
- hidden: bfloat16 [1024, 2048], P('seq', 'kv'), may hold values from -1.5 to 1.5
- in_gain: float32 [2048], replicated, may hold values from 0.5 to 1.5
- w_query: bfloat16 [2048, 2048], P(None, 'kv'), may hold values from -0.125 to 0.125
- key_projection_weight: bfloat16 [2048, 1024], P(None, 'kv'), may hold values from -0.125 to 0.125
- value_projection_weight: bfloat16 [2048, 1024], P(None, 'kv'), may hold values from -0.125 to 0.125
- w_gate: bfloat16 [2048, 16], P(None, 'kv'), may hold values from -0.125 to 0.125
- w_out: bfloat16 [2048, 2048], P('kv'), may hold values from -0.125 to 0.125
- q_gain: float32 [128], replicated, may hold values from 0.1 to 1.9
- k_gain: float32 [128], replicated, may hold values from 0.1 to 1.9
- cache_keys: bfloat16 [32768, 8, 128], P('seq', 'kv'), may hold values from -160 to 160
- pooled_cache_values: bfloat16 [32768, 8, 128], P('seq', 'kv'), may hold values from -6 to 6
- prefix_len: int32 [4], replicated, may hold values from 1024 to 8192, as said below
- own_len: int32 [32], replicated, may hold values from 256 to 2048, as said below
- request_group: int32 [32], replicated, may hold values from 0 to 3, as said below
- parents: int32 [32, 32], P('seq'), may hold values from 0 to 30, as said below
- accepted_leaf: int32 [32], P('seq'), may hold values from 0 to 31
Outputs:
- layer_out: bfloat16 [1024, 2048], P('seq', 'kv')
- accepted_keys: bfloat16 [32, 32, 1024], P('seq', None, 'kv')
- accepted_values: bfloat16 [32, 32, 1024], P('seq', None, 'kv')
Inputs may be any that keep to these rules, and one draw needn't show every extreme that they name: parents[r, 0] is 0 and node 0 is the root; for i >= 1, parents[r, i] < i. `prefix_len`: the lengths sum to 32768 // 2; one is exactly 8192 and one exactly 1024. `own_len`: the lengths sum to 32768 // 2; one is exactly 2048 and one exactly 256. `request_group`: every group holds exactly 8 requests.
All inputs are finite; a program needn't handle non-finite values.
Results may differ from a plain program's by a relative error of at most 0.017.
The roundings to bfloat16 on the way count: a program that leaves them out, or rounds other values in their place, can miss the bound.
Values may be sent and summed in bfloat16 or wider, within the bound.
A program may use at most 128 MiB of HBM per device.

v0:
```python
import math
import jax
import jax.numpy as jnp
from jax import lax
from jax.sharding import PartitionSpec as P

EPSILON = 1e-06
ROPE_BASE = 1000000.0
NEGATIVE = -1e30


def rms_scale(values, scales):
    mean_square = jnp.mean(values * values, axis=-1, keepdims=True)
    return values * lax.rsqrt(mean_square + EPSILON) * scales


def rotate_pairs(values, positions):
    half_width = values.shape[-1] // 2
    freqs = jnp.exp(
        jnp.arange(half_width, dtype=jnp.float32) * (-2.0 * math.log(ROPE_BASE) / values.shape[-1])
    )
    angles = positions[:, None] * freqs[None, :]
    cosine = jnp.concatenate([jnp.cos(angles), jnp.cos(angles)], axis=-1)[:, None, :]
    sine = jnp.concatenate([jnp.sin(angles), jnp.sin(angles)], axis=-1)[:, None, :]
    turned = jnp.concatenate([-values[..., half_width:], values[..., :half_width]], axis=-1)
    return values * cosine + turned * sine


def tree_paths(parents):
    width = parents.shape[-1]
    nodes = jnp.arange(width, dtype=jnp.int32)
    linked = (parents[:, :, None] == nodes[None, None, :]).astype(jnp.float32)
    identity_mat = jnp.eye(width, dtype=jnp.float32)
    reach = jnp.minimum(identity_mat[None] + linked * (1.0 - identity_mat[None]), 1.0)
    for squaring in range(max(1, (width - 1).bit_length())):
        reach = jnp.minimum(
            jnp.einsum("mij,mjk->mik", reach, reach, precision=lax.Precision.HIGHEST), 1.0
        )
    depth_f = jnp.sum(reach, axis=-1) - 1.0
    return (reach, depth_f)


def accepted_rows(reach, depth_f, leaves, tree_rows):
    width = reach.shape[-1]
    nodes = jnp.arange(width, dtype=jnp.int32)
    leaf_pick = (leaves[:, None] == nodes[None, :]).astype(jnp.float32)
    on_path = jnp.einsum("mi,mij->mj", leaf_pick, reach, precision=lax.Precision.HIGHEST)
    levels = (depth_f[:, None, :] == nodes.astype(jnp.float32)[None, :, None]).astype(jnp.float32)
    select = levels * on_path[:, None, :]
    return jnp.einsum(
        "mdj,mjc->mdc", select, tree_rows.astype(jnp.float32), precision=lax.Precision.HIGHEST
    ).astype(jnp.bfloat16)


def body(
    hidden,
    in_gain,
    w_query,
    key_projection_weight,
    value_projection_weight,
    w_gate,
    w_out,
    q_gain,
    k_gain,
    cache_keys,
    pooled_cache_values,
    prefix_len,
    own_len,
    request_group,
    parents,
    accepted_leaf,
):
    local_req, tree = parents.shape
    groups = prefix_len.shape[0]
    requests = own_len.shape[0]
    head_width = q_gain.shape[0]
    local_heads = w_gate.shape[1]
    local_kv = key_projection_weight.shape[1] // head_width
    per_kv = local_heads // local_kv
    local_tok = hidden.shape[0]
    pool_dev = cache_keys.shape[0]
    seq_index = lax.axis_index("seq")
    score_scale = 1.0 / math.sqrt(head_width)
    full_rows = lax.all_gather(hidden, "kv", axis=1, tiled=True)
    normed = rms_scale(full_rows.astype(jnp.float32), in_gain).astype(jnp.bfloat16)
    reach, depth_f = tree_paths(parents)
    all_reqs = jnp.arange(requests, dtype=jnp.int32)
    my_reqs = seq_index * local_req + jnp.arange(local_req, dtype=jnp.int32)
    my_pick = (my_reqs[:, None] == all_reqs[None, :]).astype(jnp.int32)
    my_group = jnp.sum(my_pick * request_group[None, :], axis=1)
    group_ids = jnp.arange(groups, dtype=jnp.int32)
    group_pick = (my_group[:, None] == group_ids[None, :]).astype(jnp.int32)
    context = jnp.sum(group_pick * prefix_len[None, :], axis=1) + jnp.sum(
        my_pick * own_len[None, :], axis=1
    )
    positions = (context[:, None].astype(jnp.float32) + depth_f).reshape(-1)
    query = jnp.dot(normed, w_query, preferred_element_type=jnp.float32).reshape(
        local_tok, local_heads, head_width
    )
    query = rotate_pairs(rms_scale(query, q_gain), positions).astype(jnp.bfloat16)
    key_new = jnp.dot(normed, key_projection_weight, preferred_element_type=jnp.float32).reshape(
        local_tok, local_kv, head_width
    )
    key_new = rotate_pairs(rms_scale(key_new, k_gain), positions).astype(jnp.bfloat16)
    value_new = (
        jnp.dot(normed, value_projection_weight, preferred_element_type=jnp.float32)
        .astype(jnp.bfloat16)
        .reshape(local_tok, local_kv, head_width)
    )
    gate_logit = jnp.dot(normed, w_gate, preferred_element_type=jnp.float32)
    tree_query = query.reshape(local_req, tree, local_kv, per_kv, head_width)
    tree_keys = key_new.reshape(local_req, tree, local_kv, head_width)
    tree_values = value_new.reshape(local_req, tree, local_kv, head_width)
    tree_scores = (
        jnp.einsum("atkgd,askd->atkgs", tree_query, tree_keys, preferred_element_type=jnp.float32)
        * score_scale
    )
    tree_seen = (reach > 0.5)[:, :, None, None, :]
    tree_scores = jnp.where(tree_seen, tree_scores, NEGATIVE)
    tree_max = jnp.max(tree_scores, axis=-1)
    tree_weights = jnp.where(tree_seen, jnp.exp(tree_scores - tree_max[..., None]), 0.0)
    tree_sum = jnp.sum(tree_weights, axis=-1).reshape(local_tok, local_heads)
    tree_num = jnp.einsum(
        "atkgs,askd->atkgd",
        tree_weights.astype(jnp.bfloat16),
        tree_values,
        preferred_element_type=jnp.float32,
    ).reshape(local_tok, local_heads, head_width)
    tree_max = tree_max.reshape(local_tok, local_heads)
    lengths_all = jnp.concatenate([prefix_len, own_len])
    starts = jnp.cumsum(lengths_all) - lengths_all
    slot_ids = seq_index * pool_dev + jnp.arange(pool_dev, dtype=jnp.int32)
    slot_segment = jnp.sum((starts[None, :] <= slot_ids[:, None]).astype(jnp.int32), axis=1) - 1
    block_len = min(512, pool_dev)
    block_count = pool_dev // block_len
    key_blocks = cache_keys.reshape(block_count, block_len, local_kv, head_width)
    value_blocks = pooled_cache_values.reshape(block_count, block_len, local_kv, head_width)
    segment_blocks = slot_segment.reshape(block_count, block_len)
    query_flat = query.reshape(local_tok, local_heads * head_width)
    query_piece = lax.all_gather(query_flat, "seq", axis=0, tiled=True)
    row_ids = jnp.arange(query_piece.shape[0], dtype=jnp.int32)
    owners = row_ids // tree
    count = query_piece.shape[0]
    grouped = query_piece.reshape(count, local_kv, per_kv, head_width)
    owner_pick = (owners[:, None] == all_reqs[None, :]).astype(jnp.int32)
    known = owners >= 0
    prefix_segment = jnp.where(known, jnp.sum(owner_pick * request_group[None, :], axis=1), -5)
    own_segment = jnp.where(known, owners + groups, -5)

    def visit(carry, block):
        run_max, run_sum, run_num = carry
        keys_block, values_block, segment_block = block
        scores = (
            jnp.einsum("nkgd,pkd->nkgp", grouped, keys_block, preferred_element_type=jnp.float32)
            * score_scale
        )
        visible = (segment_block[None, :] == prefix_segment[:, None]) | (
            segment_block[None, :] == own_segment[:, None]
        )
        visible = visible[:, None, None, :]
        scores = jnp.where(visible, scores, NEGATIVE)
        new_max = jnp.maximum(run_max, jnp.max(scores, axis=-1))
        weights = jnp.where(visible, jnp.exp(scores - new_max[..., None]), 0.0)
        factor = jnp.exp(run_max - new_max)
        run_sum = run_sum * factor + jnp.sum(weights, axis=-1)
        run_num = run_num * factor[..., None] + jnp.einsum(
            "nkgp,pkd->nkgd",
            weights.astype(jnp.bfloat16),
            values_block,
            preferred_element_type=jnp.float32,
        )
        return ((new_max, run_sum, run_num), None)

    start_state = (
        jnp.full((count, local_kv, per_kv), NEGATIVE, jnp.float32),
        jnp.zeros((count, local_kv, per_kv), jnp.float32),
        jnp.zeros((count, local_kv, per_kv, head_width), jnp.float32),
    )
    final_state, unused = lax.scan(visit, start_state, (key_blocks, value_blocks, segment_blocks))
    run_max, run_sum, run_num = final_state
    part_max = run_max.reshape(count, local_heads)
    part_sum = run_sum.reshape(count, local_heads)
    part_num = run_num.reshape(count, local_heads * head_width)
    all_rows = part_max.shape[0]
    cache_max = lax.pmax(part_max.astype(jnp.bfloat16), "seq").astype(part_max.dtype)
    factor = jnp.exp(part_max - cache_max)
    scaled_num = (part_num.reshape(all_rows, local_heads, head_width) * factor[..., None]).reshape(
        all_rows, local_heads * head_width
    )
    summed_num, summed_sum = (
        lax.psum_scatter(
            scaled_num.astype(jnp.bfloat16), "seq", scatter_dimension=0, tiled=True
        ).astype(jnp.float32),
        lax.psum_scatter(
            (part_sum * factor).astype(jnp.bfloat16), "seq", scatter_dimension=0, tiled=True
        ).astype(jnp.float32),
    )
    own_max = lax.dynamic_slice_in_dim(cache_max, seq_index * local_tok, local_tok, 0)
    final_max = jnp.maximum(own_max, tree_max)
    cache_factor = jnp.exp(own_max - final_max)
    tree_factor = jnp.exp(tree_max - final_max)
    weight_sum = summed_sum * cache_factor + tree_sum * tree_factor
    mixed = (
        summed_num.reshape(local_tok, local_heads, head_width) * cache_factor[..., None]
        + tree_num * tree_factor[..., None]
    )
    mixed = mixed / weight_sum[..., None]
    attended = (
        (mixed * jax.nn.sigmoid(gate_logit)[..., None])
        .astype(jnp.bfloat16)
        .reshape(local_tok, local_heads * head_width)
    )
    projected = jnp.dot(attended, w_out, preferred_element_type=jnp.float32)
    layer_part = lax.psum_scatter(
        projected.astype(jnp.bfloat16), "kv", scatter_dimension=1, tiled=True
    ).astype(jnp.float32)
    layer_out = (layer_part + hidden.astype(jnp.float32)).astype(jnp.bfloat16)
    tree_rows = jnp.concatenate(
        [
            key_new.reshape(local_req, tree, local_kv * head_width),
            value_new.reshape(local_req, tree, local_kv * head_width),
        ],
        axis=-1,
    )
    picked = accepted_rows(reach, depth_f, accepted_leaf, tree_rows)
    accepted_keys = picked[:, :, : local_kv * head_width]
    accepted_values = picked[:, :, local_kv * head_width :]
    return (layer_out, accepted_keys, accepted_values)


def solution(mesh):
    in_specs = (
        P("seq", "kv"),
        P(),
        P(None, "kv"),
        P(None, "kv"),
        P(None, "kv"),
        P(None, "kv"),
        P("kv", None),
        P(),
        P(),
        P("seq", "kv", None),
        P("seq", "kv", None),
        P(),
        P(),
        P(),
        P("seq", None),
        P("seq"),
    )
    out_specs = (P("seq", "kv"), P("seq", None, "kv"), P("seq", None, "kv"))
    return jax.shard_map(body, mesh=mesh, in_specs=in_specs, out_specs=out_specs, check_vma=False)
```

profile of v0, /device:TPU:0, one launch (start us, length us, event | category | flops | bytes accessed | tf_op | source)
XLA Modules:
  0.0 365.4 jit_solution(637547949621892404)
XLA Ops:
  8.1 7.4 %all_gather.6 = bf16[64,2048]{1,0:T(8,128)(2,1)S(1)} all-gather(bf16[64,1024]{1,0:T(8,128)(2,1)} %param.18), channel_id=1, replica_groups=mesh['kv'=2,'seq'=16] {'kv'}, dimensions={1}, use_global_device_ids=true | all-gather | bytes 393216 | tf_op jit(solution)/shard_map/all_gather | solution.py:84
  15.6 3.1 fusion.96
  26.7 39.9 %all-gather.2.cloned.1.call-done = bf16[1024,1024]{1,0:T(8,128)(2,1)} async-done(((bf16[64,1024]{1,0:T(8,128)(2,1)}), bf16[1024,1024]{1,0:T(8,128)(2,1)}) %all-gather.2.cloned.1.call-update) | async-done | bytes 2097168 | tf_op jit(solution)/shard_map/all_gather | solution.py:140
  66.6 4.5 %reshape.343 = bf16[1024,4,2,128]{3,2,1,0:T(2,128)(2,1)} reshape(bf16[1024,1024]{1,0:T(8,128)(2,1)} %all-gather.2.cloned.1.call-done) | data formatting | bytes 4194304 | tf_op jit(solution)/shard_map/reshape | solution.py:144
  71.1 3.2 copy.172
  74.3 84.1 %while.15 = (s32[]{:T(128)}, f32[1024,4,2]{0,2,1:T(2,128)S(1)}, f32[1024,4,2]{0,2,1:T(2,128)S(1)}, f32[1024,4,2,128]{0,3,2,1:T(8,128)}, s32[4,512]{1,0:T(4,128)S...) while((s32[]{:T(128)}, f32[1024,4,2]{0,2,1:T(2,128)S(1)}, ...), condition=%wide.region_12.13_spmd.clone, body=%wide.region_9.12_spmd.clone.sunk | while | flops 2206780416 | bytes 69748896 | solution.py:179
  78.2 4.6 %fusion.137 = (f32[1024,4,2]{0,2,1:T(2,128)S(1)}, f32[4,512,1024,2]{2,1,3,0:T(8,128)S(1)}) fusion(pred[1024,512]{0,1:T(8,128)(4,1)S(1)} %compare_or_fusion.2, bf16[1024,4,2,128]{3,0,2,1:T(8,128)(2,1)} %get-tuple-element.291, bf16[1,512,4,128]{3,2,1,0:T(4,128)(2,1)} %get-tuple-element.256), kind=kOutput, calls=%fused_computation.3.clone.1 | convolution fusion | flops 1086316544 | bytes 19955712 | tf_op jit(solution)/shard_map/while/body/eval_jaxpr/nkgd,pkd->nkgp/dot_general | solution.py:154
  82.8 4.1 %fusion.139 = f32[1024,4,2]{0,2,1:T(2,128)S(1)} fusion(f32[4,512,1024,2]{2,1,3,0:T(8,128)S(1)} %get-tuple-element.258, f32[1024,4,2]{0,2,1:T(2,128)S(1)} %fusion.138, pred[1024,512]{0,1:T(8,128)(4,1)S(1)} %compare_or_fusion.2), kind=kLoop, calls=%fused_computation.5.clone.1 | loop fusion | flops 20963328 | bytes 17367040 | tf_op jit(solution)/shard_map/while/body/eval_jaxpr/reduce_sum | solution.py:165
  87.0 7.1 %bitcast_add_fusion.2 = f32[1024,4,2,128]{0,3,2,1:T(8,128)} fusion(f32[1024,4,2,128]{0,3,2,1:T(8,128)} %get-tuple-element.276, f32[4,512,1024,2]{2,1,3,0:T(8,128)S(1)} %get-tuple-element.258, f32[1024,4,2]{0,2,1:T(2,128)S(1)} %fusion.138, pred[1024,512]{0,1:T(8,128)(4,1)S(1)} %compare_or_fusion.2, f32[1024,4,2]{0,2,1:T(2,128)S(1)} %get-tuple-element.260, ...), kind=kOutput, calls=%fused_computation.8.clone.1 | convolution fusion | flops 1097859072 | bytes 26279936 | tf_op jit(solution)/shard_map/while/body/eval_jaxpr/nkgp,pkd->nkgd/dot_general | solution.py:166
  98.1 4.6 %fusion.137 = (f32[1024,4,2]{0,2,1:T(2,128)S(1)}, f32[4,512,1024,2]{2,1,3,0:T(8,128)S(1)}) fusion(pred[1024,512]{0,1:T(8,128)(4,1)S(1)} %compare_or_fusion.2, bf16[1024,4,2,128]{3,0,2,1:T(8,128)(2,1)} %get-tuple-element.291, bf16[1,512,4,128]{3,2,1,0:T(4,128)(2,1)} %get-tuple-element.256), kind=kOutput, calls=%fused_computation.3.clone.1 | convolution fusion | flops 1086316544 | bytes 19955712 | tf_op jit(solution)/shard_map/while/body/eval_jaxpr/nkgd,pkd->nkgp/dot_general | solution.py:154
  102.7 4.1 %fusion.139 = f32[1024,4,2]{0,2,1:T(2,128)S(1)} fusion(f32[4,512,1024,2]{2,1,3,0:T(8,128)S(1)} %get-tuple-element.258, f32[1024,4,2]{0,2,1:T(2,128)S(1)} %fusion.138, pred[1024,512]{0,1:T(8,128)(4,1)S(1)} %compare_or_fusion.2), kind=kLoop, calls=%fused_computation.5.clone.1 | loop fusion | flops 20963328 | bytes 17367040 | tf_op jit(solution)/shard_map/while/body/eval_jaxpr/reduce_sum | solution.py:165
  106.9 8.7 %bitcast_add_fusion.2 = f32[1024,4,2,128]{0,3,2,1:T(8,128)} fusion(f32[1024,4,2,128]{0,3,2,1:T(8,128)} %get-tuple-element.276, f32[4,512,1024,2]{2,1,3,0:T(8,128)S(1)} %get-tuple-element.258, f32[1024,4,2]{0,2,1:T(2,128)S(1)} %fusion.138, pred[1024,512]{0,1:T(8,128)(4,1)S(1)} %compare_or_fusion.2, f32[1024,4,2]{0,2,1:T(2,128)S(1)} %get-tuple-element.260, ...), kind=kOutput, calls=%fused_computation.8.clone.1 | convolution fusion | flops 1097859072 | bytes 26279936 | tf_op jit(solution)/shard_map/while/body/eval_jaxpr/nkgp,pkd->nkgd/dot_general | solution.py:166
  119.5 4.6 %fusion.137 = (f32[1024,4,2]{0,2,1:T(2,128)S(1)}, f32[4,512,1024,2]{2,1,3,0:T(8,128)S(1)}) fusion(pred[1024,512]{0,1:T(8,128)(4,1)S(1)} %compare_or_fusion.2, bf16[1024,4,2,128]{3,0,2,1:T(8,128)(2,1)} %get-tuple-element.291, bf16[1,512,4,128]{3,2,1,0:T(4,128)(2,1)} %get-tuple-element.256), kind=kOutput, calls=%fused_computation.3.clone.1 | convolution fusion | flops 1086316544 | bytes 19955712 | tf_op jit(solution)/shard_map/while/body/eval_jaxpr/nkgd,pkd->nkgp/dot_general | solution.py:154
  124.1 4.1 %fusion.139 = f32[1024,4,2]{0,2,1:T(2,128)S(1)} fusion(f32[4,512,1024,2]{2,1,3,0:T(8,128)S(1)} %get-tuple-element.258, f32[1024,4,2]{0,2,1:T(2,128)S(1)} %fusion.138, pred[1024,512]{0,1:T(8,128)(4,1)S(1)} %compare_or_fusion.2), kind=kLoop, calls=%fused_computation.5.clone.1 | loop fusion | flops 20963328 | bytes 17367040 | tf_op jit(solution)/shard_map/while/body/eval_jaxpr/reduce_sum | solution.py:165
  128.3 8.7 %bitcast_add_fusion.2 = f32[1024,4,2,128]{0,3,2,1:T(8,128)} fusion(f32[1024,4,2,128]{0,3,2,1:T(8,128)} %get-tuple-element.276, f32[4,512,1024,2]{2,1,3,0:T(8,128)S(1)} %get-tuple-element.258, f32[1024,4,2]{0,2,1:T(2,128)S(1)} %fusion.138, pred[1024,512]{0,1:T(8,128)(4,1)S(1)} %compare_or_fusion.2, f32[1024,4,2]{0,2,1:T(2,128)S(1)} %get-tuple-element.260, ...), kind=kOutput, calls=%fused_computation.8.clone.1 | convolution fusion | flops 1097859072 | bytes 26279936 | tf_op jit(solution)/shard_map/while/body/eval_jaxpr/nkgp,pkd->nkgd/dot_general | solution.py:166
  140.9 4.6 %fusion.137 = (f32[1024,4,2]{0,2,1:T(2,128)S(1)}, f32[4,512,1024,2]{2,1,3,0:T(8,128)S(1)}) fusion(pred[1024,512]{0,1:T(8,128)(4,1)S(1)} %compare_or_fusion.2, bf16[1024,4,2,128]{3,0,2,1:T(8,128)(2,1)} %get-tuple-element.291, bf16[1,512,4,128]{3,2,1,0:T(4,128)(2,1)} %get-tuple-element.256), kind=kOutput, calls=%fused_computation.3.clone.1 | convolution fusion | flops 1086316544 | bytes 19955712 | tf_op jit(solution)/shard_map/while/body/eval_jaxpr/nkgd,pkd->nkgp/dot_general | solution.py:154
  145.5 4.1 %fusion.139 = f32[1024,4,2]{0,2,1:T(2,128)S(1)} fusion(f32[4,512,1024,2]{2,1,3,0:T(8,128)S(1)} %get-tuple-element.258, f32[1024,4,2]{0,2,1:T(2,128)S(1)} %fusion.138, pred[1024,512]{0,1:T(8,128)(4,1)S(1)} %compare_or_fusion.2), kind=kLoop, calls=%fused_computation.5.clone.1 | loop fusion | flops 20963328 | bytes 17367040 | tf_op jit(solution)/shard_map/while/body/eval_jaxpr/reduce_sum | solution.py:165
  149.7 8.7 %bitcast_add_fusion.2 = f32[1024,4,2,128]{0,3,2,1:T(8,128)} fusion(f32[1024,4,2,128]{0,3,2,1:T(8,128)} %get-tuple-element.276, f32[4,512,1024,2]{2,1,3,0:T(8,128)S(1)} %get-tuple-element.258, f32[1024,4,2]{0,2,1:T(2,128)S(1)} %fusion.138, pred[1024,512]{0,1:T(8,128)(4,1)S(1)} %compare_or_fusion.2, f32[1024,4,2]{0,2,1:T(2,128)S(1)} %get-tuple-element.260, ...), kind=kOutput, calls=%fused_computation.8.clone.1 | convolution fusion | flops 1097859072 | bytes 26279936 | tf_op jit(solution)/shard_map/while/body/eval_jaxpr/nkgp,pkd->nkgd/dot_general | solution.py:166
  158.4 5.4 %copy.208 = f32[1024,1024]{1,0:T(8,128)} copy(f32[1024,1024]{0,1:T(8,128)} %bitcast.172) | data formatting | bytes 8388608 | tf_op jit(solution)/shard_map/reshape;reshape | solution.py:187
  163.8 59.5 %pmax.7 = bf16[1024,8]{0,1:T(8,128)(2,1)S(1)} all-reduce(bf16[1024,8]{0,1:T(8,128)(2,1)S(1)} %convert_element_type.109), channel_id=1, replica_groups=mesh['kv'=2,'seq'=16] {'seq'}, use_global_device_ids=true, to_apply=%region_13.14 | all-reduce | flops 8192 | bytes 32768 | tf_op jit(solution)/shard_map/pmax | solution.py:185
  251.4 25.6 %reduce-scatter.10.cloned.1.call-done = bf16[64,8]{1,0:T(8,128)(2,1)} async-done(((bf16[1024,8]{1,0:T(8,128)(2,1)}), bf16[64,8]{1,0:T(8,128)(2,1)}) %reduce-scatter.10.cloned.1.call-update) | async-done | bytes 1040
  278.1 63.2 %reduce-scatter.6.cloned.1.call-done = bf16[64,1024]{1,0:T(8,128)(2,1)} async-done(((bf16[1024,1024]{1,0:T(8,128)(2,1)}), bf16[64,1024]{1,0:T(8,128)(2,1)}) %reduce-scatter.6.cloned.1.call-update) | async-done | bytes 131088 | tf_op jit(solution)/shard_map/reduce_scatter | solution.py:191
  342.6 3.9 %convolution_convert_fusion = bf16[64,2048]{1,0:T(8,128)(2,1)} fusion(bf16[1024,2048]{1,0:T(8,128)(2,1)} %param.24, f32[8,8,8,128]{3,2,1,0:T(8,128)S(1)} %bitcast.180, f32[8,8,8,128]{3,2,1,0:T(8,128)S(1)} %bitcast.183, f32[64,1024]{1,0:T(8,128)S(1)} %reshape.350, f32[8,8,8,128]{3,2,1,0:T(8,128)S(1)} %bitcast.181, f32[8,8,8,128]{3,2,1,0:T(8,128)S(1)} %bitcast.182, ...), kind=kOutput, calls=%fused_computation.37 | convolution fusion | flops 269025280 | bytes 5898240 | tf_op jit(solution)/shard_map/dot_general | solution.py:213
  347.5 9.8 %reduce-scatter.8.cloned.1.call-done = bf16[64,1024]{1,0:T(8,128)(2,1)} async-done(((bf16[64,2048]{1,0:T(8,128)(2,1)}), bf16[64,1024]{1,0:T(8,128)(2,1)}) %reduce-scatter.8.cloned.1.call-update) | async-done | bytes 131088 | tf_op jit(solution)/shard_map/reduce_scatter | solution.py:214
  (215 shorter events, 57.5 us)
Async XLA Ops:
  7.2 17.1 %copy-start = (bf16[2048,512]{1,0:T(8,128)(2,1)S(1)}, bf16[2048,512]{1,0:T(8,128)(2,1)}, u32[]{:S(2)}) copy-start(bf16[2048,512]{1,0:T(8,128)(2,1)} %param.21) | copy-start | bytes 6291460
  7.2 11.9 %copy-start.21 = (f32[128]{0:T(128)S(1)}, f32[128]{0:T(128)}, u32[]{:S(2)}) copy-start(f32[128]{0:T(128)} %param.25) | copy-start | bytes 1540
  7.2 12.1 %copy-start.28 = (s32[2,32]{1,0:T(2,128)S(1)}, s32[2,32]{1,0:T(2,128)}, u32[]{:S(2)}) copy-start(s32[2,32]{1,0:T(2,128)} %param.32) | copy-start | bytes 772
  7.2 13.1 %copy-start.27 = (s32[32]{0:T(128)S(1)}, s32[32]{0:T(128)}, u32[]{:S(2)}) copy-start(s32[32]{0:T(128)} %param.30) | copy-start | bytes 388
  7.2 13.1 %copy-start.26 = (s32[32]{0:T(128)S(1)}, s32[32]{0:T(128)}, u32[]{:S(2)}) copy-start(s32[32]{0:T(128)} %param.31) | copy-start | bytes 388
  7.2 13.3 %copy-start.29 = (s32[4]{0:T(128)S(1)}, s32[4]{0:T(128)}, u32[]{:S(2)}) copy-start(s32[4]{0:T(128)} %param.29) | copy-start | bytes 52
  7.2 59.4 %all-gather.2.cloned.1.call-start = ((), (), s32[]{:S(2)}) async-start(), calls=%async_computation.3 | async-start | bytes 2228224 | tf_op jit(solution)/shard_map/all_gather | solution.py:140
  7.3 14.6 %copy-start.25 = (f32[64]{0:T(128)}, f32[64]{0:T(128)S(1)}, u32[]{:S(2)}) copy-start(f32[64]{0:T(128)S(1)} %multiply_exponential_fusion) | copy-start | bytes 772
  15.5 10.3 %copy-start.3 = (bf16[64,2048]{1,0:T(8,128)(2,1)}, bf16[64,2048]{1,0:T(8,128)(2,1)S(1)}, u32[]{:S(2)}) copy-start(bf16[64,2048]{1,0:T(8,128)(2,1)S(1)} %all_gather.6) | copy-start | bytes 786436
  15.6 10.2 %copy-start.22 = (f32[64]{0:T(128)}, f32[64]{0:T(128)S(1)}, u32[]{:S(2)}) copy-start(f32[64]{0:T(128)S(1)} %add_rsqrt_fusion.2) | copy-start | bytes 772
  15.6 8.6 %copy-start.19 = (f32[2048]{0:T(1024)S(1)}, f32[2048]{0:T(1024)}, u32[]{:S(2)}) copy-start(f32[2048]{0:T(1024)} %param.19) | copy-start | bytes 24580
  20.3 50.7 %copy-start.15 = (f32[2,32,32]{2,1,0:T(8,128)}, f32[2,32,32]{2,1,0:T(8,128)S(1)}, u32[]{:S(2)}) copy-start(f32[2,32,32]{2,1,0:T(8,128)S(1)} %get-tuple-element.190) | copy-start | bytes 24580
  21.3 49.8 %copy-start.24 = (f32[2,32]{1,0:T(2,128)}, f32[2,32]{1,0:T(2,128)S(1)}, u32[]{:S(2)}) copy-start(f32[2,32]{1,0:T(2,128)S(1)} %get-tuple-element.186) | copy-start | bytes 772
  23.6 253.4 %reduce-scatter.10.cloned.1.call-start = ((), (), s32[]{:S(2)}) async-start(), calls=%async_computation.6 | async-start | bytes 278528
  24.8 49.5 %copy-start.5 = (f32[64,512]{1,0:T(8,128)}, f32[64,512]{1,0:T(8,128)S(1)}, u32[]{:S(2)}) copy-start(f32[64,512]{1,0:T(8,128)S(1)} %fusion.94) | copy-start | bytes 393220
  224.2 117.1 %reduce-scatter.6.cloned.1.call-start = ((), (), s32[]{:S(2)}) async-start(), calls=%async_computation.4 | async-start | bytes 2228224 | tf_op jit(solution)/shard_map/reduce_scatter | solution.py:191
  226.9 9.5 %copy-start.4 = (bf16[64,2048]{1,0:T(8,128)(2,1)S(1)}, bf16[64,2048]{1,0:T(8,128)(2,1)}, u32[]{:S(2)}) copy-start(bf16[64,2048]{1,0:T(8,128)(2,1)} %copy-done.3) | copy-start | bytes 786436
  229.0 14.5 %copy-start.8 = (f32[64,8,64]{2,0,1:T(8,128)S(1)}, f32[64,8,64]{2,0,1:T(8,128)}, u32[]{:S(2)}) copy-start(f32[64,8,64]{2,0,1:T(8,128)} %copy-done.7) | copy-start | bytes 393220
  229.0 14.5 %copy-start.10 = (f32[64,8,64]{2,0,1:T(8,128)S(1)}, f32[64,8,64]{2,0,1:T(8,128)}, u32[]{:S(2)}) copy-start(f32[64,8,64]{2,0,1:T(8,128)} %copy-done.9) | copy-start | bytes 393220
  229.0 128.3 %reduce-scatter.8.cloned.1.call-start = ((), (), s32[]{:S(2)}) async-start(), calls=%async_computation.5 | async-start | bytes 393216 | tf_op jit(solution)/shard_map/reduce_scatter | solution.py:214
  232.1 9.6 %copy-start.17 = (f32[64,128]{1,0:T(8,128)S(1)}, f32[64,128]{1,0:T(8,128)}, u32[]{:S(2)}) copy-start(f32[64,128]{1,0:T(8,128)} %copy-done.16) | copy-start | bytes 98308
  247.1 99.4 %copy-start.12 = (bf16[64,512]{1,0:T(8,128)(2,1)S(1)}, bf16[64,512]{1,0:T(8,128)(2,1)}, u32[]{:S(2)}) copy-start(bf16[64,512]{1,0:T(8,128)(2,1)} %copy-done.11) | copy-start | bytes 196612
  247.1 99.4 %copy-start.23 = (f32[2,32]{1,0:T(2,128)S(1)}, f32[2,32]{1,0:T(2,128)}, u32[]{:S(2)}) copy-start(f32[2,32]{1,0:T(2,128)} %get-tuple-element.185) | copy-start | bytes 772
  251.4 105.9 %copy-start.13 = (bf16[64,1024]{1,0:T(8,128)(2,1)S(1)}, bf16[64,1024]{1,0:T(8,128)(2,1)}, u32[]{:S(2)}) copy-start(bf16[64,1024]{1,0:T(8,128)(2,1)} %param.18) | copy-start | bytes 393220
  (14 other events, 36.7 us)
Sparse Core Ops, SparseCore 0:
  23.7 42.8 all-gather.1
  224.3 52.5 reduce-scatter.9
  280.7 60.5 reduce-scatter.5
  346.6 10.6 reduce-scatter.7
where the time goes:
time: 367 us; the launch traced here: 365 us
  waiting for transfers between devices  139 us (38%)
  blocking collectives  66.8 us (18%)
  matrix products  66.7 us (18%)
  local copies, waits for them, and re-layouts  47.5 us (13%)
  other arithmetic  30.8 us (8%)
  between operations  14.5 us (4%)
    reduce_scatter x1, waiting for transfers between devices, body(): lax.psum_scatter(scaled_num.astype(jnp.bfloat16), 'seq', scatter_dimensio...  63.2 us
    pmax x1, blocking collectives, body(): lax.pmax(part_max.astype(jnp.bfloat16), 'seq').astype(part_max.dtype)  59.5 us
    all_gather x1, waiting for transfers between devices, body(): query_piece = lax.all_gather(query_flat, 'seq', axis=0, tiled=True)  39.9 us
    dot_general x4, matrix products, visit(): jnp.einsum('nkgp,pkd->nkgd', weights.astype(jnp.bfloat16), values_block,...  33.2 us
    unnamed x5, waiting for transfers between devices  25.6 us
    dot_general x4, matrix products, visit(): jnp.einsum('nkgd,pkd->nkgp', grouped, keys_block, preferred_element_type=...  18.3 us
    reduce_sum x4, other arithmetic, visit(): run_sum = run_sum * factor + jnp.sum(weights, axis=-1)  16.3 us
    dynamic_slice x12, local copies, waits for them, and re-layouts, body(): lax.scan(visit, start_state, (key_blocks, value_blocks, segment_blocks))  14 us
  transfers between devices with their start and end apart: 4, of which 4 were waited for; matrix products, arithmetic and copies ran while one was open for 8% of the time, Pallas kernels for 0%

commit v1 on v0

--- a/solution.py
+++ b/solution.py
@@ -7,6 +7,28 @@
 EPSILON = 1e-06
 ROPE_BASE = 1000000.0
 NEGATIVE = -1e30
+
+
+def laid_out(pieces, dim):
+    pieces = jnp.moveaxis(pieces, 0, dim)
+    lengths = pieces.shape
+    return pieces.reshape(*lengths[:dim], lengths[dim] * lengths[dim + 1], *lengths[dim + 2 :])
+
+
+def gather_around(x, axis, dim):
+    size = lax.axis_size(axis)
+    pairs = [(i, (i + 1) % size) for i in range(size)]
+    back = [(b, a) for a, b in pairs]
+    lower, upper = ([], [])
+    for turn in range(size - 1):
+        if turn % 2 == 0:
+            lower.append(lax.ppermute(lower[-1] if lower else x, axis, pairs))
+        else:
+            upper.append(lax.ppermute(upper[-1] if upper else x, axis, back))
+    pieces = jnp.stack([*lower[::-1], x, *upper])
+    shift = lax.axis_index(axis) - len(lower)
+    pieces = pieces[(jnp.arange(size) - shift) % size]
+    return laid_out(pieces, dim)
 
 
 def rms_scale(values, scales):
@@ -137,7 +159,7 @@
     value_blocks = pooled_cache_values.reshape(block_count, block_len, local_kv, head_width)
     segment_blocks = slot_segment.reshape(block_count, block_len)
     query_flat = query.reshape(local_tok, local_heads * head_width)
-    query_piece = lax.all_gather(query_flat, "seq", axis=0, tiled=True)
+    query_piece = gather_around(query_flat, "seq", 0)
     row_ids = jnp.arange(query_piece.shape[0], dtype=jnp.int32)
     owners = row_ids // tree
     count = query_piece.shape[0]

time: 367 us -> 392 us (1.068)
  starting transfers between devices: 0.34 us -> 31 us
  other arithmetic: 30.8 us -> 26.4 us
    all_gather x1 -> x0, waiting for transfers between devices: 39.9 us -> none  [body(): query_piece = lax.all_gather(query_flat, 'seq', axis=0, tiled=True)]
    ppermute x0 -> x15, starting transfers between devices: none -> 30.6 us  [the longest x7 30.6 us: gather_around(): upper.append(lax.ppermute(upper[-1] if upper else x, axis, back))]
    ppermute x0 -> x15, waiting for transfers between devices: none -> 26.4 us  [the longest x8 26.4 us: gather_around(): lower.append(lax.ppermute(lower[-1] if lower else x, axis, pairs))]
    unnamed x5 -> x4, waiting for transfers between devices: 25.6 us -> 41.7 us
    unnamed x66 -> x89, local copies, waits for them, and re-layouts: 8.05 us -> 16.2 us
    reshape x1 -> x0, local copies, waits for them, and re-layouts: 4.48 us -> none  [body(): grouped = query_piece.reshape(count, local_kv, per_kv, head_width)]
  transfers between devices with their start and end apart: 4 -> 18, of which waited for: 4 -> 11; matrix products, arithmetic and copies ran while one was open for 8% -> 6% of each run, Pallas kernels for 0% -> 0%
where the time goes in v1:
time: 392 us
  waiting for transfers between devices  141 us (36%)
  blocking collectives  65 us (17%)
  matrix products  63.4 us (16%)
  local copies, waits for them, and re-layouts  49.8 us (13%)
  starting transfers between devices  31 us (8%)
  other arithmetic  26.4 us (7%)
  between operations  14.6 us (4%)
    reduce_scatter x1, waiting for transfers between devices, body(): lax.psum_scatter(scaled_num.astype(jnp.bfloat16), 'seq', scatter_dimensio...  63.3 us
    pmax x1, blocking collectives, body(): lax.pmax(part_max.astype(jnp.bfloat16), 'seq').astype(part_max.dtype)  57.6 us
    unnamed x4, waiting for transfers between devices  41.7 us
    dot_general x4, matrix products, visit(): jnp.einsum('nkgp,pkd->nkgd', weights.astype(jnp.bfloat16), values_block,...  33.3 us
    ppermute x7, starting transfers between devices, gather_around(): upper.append(lax.ppermute(upper[-1] if upper else x, axis, back))  30.6 us
    ppermute x8, waiting for transfers between devices, gather_around(): lower.append(lax.ppermute(lower[-1] if lower else x, axis, pairs))  26.4 us
    dot_general x4, matrix products, visit(): jnp.einsum('nkgd,pkd->nkgp', grouped, keys_block, preferred_element_type=...  17.3 us
    reduce_sum x4, other arithmetic, visit(): run_sum = run_sum * factor + jnp.sum(weights, axis=-1)  16.3 us
  transfers between devices with their start and end apart: 18, of which 11 were waited for; matrix products, arithmetic and copies ran while one was open for 6% of the time, Pallas kernels for 0%

profile of v1, /device:TPU:0, one launch (start us, length us, event | category | flops | bytes accessed | tf_op | source)
XLA Modules:
  0.0 391.7 jit_solution(12325708596908857779)
XLA Ops:
  8.1 7.4 %all_gather.3 = bf16[64,2048]{1,0:T(8,128)(2,1)S(1)} all-gather(bf16[64,1024]{1,0:T(8,128)(2,1)} %param.18), channel_id=1, replica_groups=mesh['kv'=2,'seq'=16] {'kv'}, dimensions={1}, use_global_device_ids=true | all-gather | bytes 393216 | tf_op jit(solution)/shard_map/all_gather | solution.py:106
  28.4 5.3 %collective-permute-done = bf16[64,1024]{1,0:T(8,128)(2,1)S(1)} collective-permute-done((bf16[64,1024]{1,0:T(8,128)(2,1)S(1)}, bf16[64,1024]{1,0:T(8,128)(2,1)S(1)}, u32[]{:S(2)}, u32[]{:S(2)}) %collective-permute-start) | collective-permute-done | bytes 131104 | tf_op jit(solution)/shard_map/ppermute | solution.py:25
  34.2 6.6 %collective-permute-done.1 = bf16[64,1024]{1,0:T(8,128)(2,1)S(1)} collective-permute-done((bf16[64,1024]{1,0:T(8,128)(2,1)S(1)}, bf16[64,1024]{1,0:T(8,128)(2,1)S(1)}, u32[]{:S(2)}, u32[]{:S(2)}) %collective-permute-start.1) | collective-permute-done | bytes 131104 | tf_op jit(solution)/shard_map/ppermute | solution.py:25
  40.9 4.4 %collective-permute-start.9 = (bf16[64,1024]{1,0:T(8,128)(2,1)S(1)}, bf16[64,1024]{1,0:T(8,128)(2,1)S(1)}, u32[]{:S(2)}, u32[]{:S(2)}) collective-permute-start(bf16[64,1024]{1,0:T(8,128)(2,1)S(1)} %collective-permute-done.8), channel_id=1, source_target_pairs={{1,0},{2,1},{3,2},{4,3},{5,4},{6,5},{7,6},{8,7},{9,8},{10,9},{11,1... | collective-permute-start | bytes 393224 | tf_op jit(solution)/shard_map/ppermute | solution.py:27
  48.2 4.5 %collective-permute-start.10 = (bf16[64,1024]{1,0:T(8,128)(2,1)S(1)}, bf16[64,1024]{1,0:T(8,128)(2,1)S(1)}, u32[]{:S(2)}, u32[]{:S(2)}) collective-permute-start(bf16[64,1024]{1,0:T(8,128)(2,1)S(1)} %collective-permute-done.9), channel_id=1, source_target_pairs={{1,0},{2,1},{3,2},{4,3},{5,4},{6,5},{7,6},{8,7},{9,8},{10,9},{11,1... | collective-permute-start | bytes 393224 | tf_op jit(solution)/shard_map/ppermute | solution.py:27
  55.2 4.6 %collective-permute-start.11 = (bf16[64,1024]{1,0:T(8,128)(2,1)S(1)}, bf16[64,1024]{1,0:T(8,128)(2,1)S(1)}, u32[]{:S(2)}, u32[]{:S(2)}) collective-permute-start(bf16[64,1024]{1,0:T(8,128)(2,1)S(1)} %collective-permute-done.10), channel_id=1, source_target_pairs={{1,0},{2,1},{3,2},{4,3},{5,4},{6,5},{7,6},{8,7},{9,8},{10,9},{11,1... | collective-permute-start | bytes 393224 | tf_op jit(solution)/shard_map/ppermute | solution.py:27
  62.5 4.5 %collective-permute-start.12 = (bf16[64,1024]{1,0:T(8,128)(2,1)S(1)}, bf16[64,1024]{1,0:T(8,128)(2,1)S(1)}, u32[]{:S(2)}, u32[]{:S(2)}) collective-permute-start(bf16[64,1024]{1,0:T(8,128)(2,1)S(1)} %collective-permute-done.11), channel_id=1, source_target_pairs={{1,0},{2,1},{3,2},{4,3},{5,4},{6,5},{7,6},{8,7},{9,8},{10,9},{11,1... | collective-permute-start | bytes 393224 | tf_op jit(solution)/shard_map/ppermute | solution.py:27
  69.8 4.5 %collective-permute-start.13 = (bf16[64,1024]{1,0:T(8,128)(2,1)S(1)}, bf16[64,1024]{1,0:T(8,128)(2,1)S(1)}, u32[]{:S(2)}, u32[]{:S(2)}) collective-permute-start(bf16[64,1024]{1,0:T(8,128)(2,1)S(1)} %collective-permute-done.12), channel_id=1, source_target_pairs={{1,0},{2,1},{3,2},{4,3},{5,4},{6,5},{7,6},{8,7},{9,8},{10,9},{11,1... | collective-permute-start | bytes 393224 | tf_op jit(solution)/shard_map/ppermute | solution.py:27
  77.5 4.7 %collective-permute-start.14 = (bf16[64,1024]{1,0:T(8,128)(2,1)S(1)}, bf16[64,1024]{1,0:T(8,128)(2,1)S(1)}, u32[]{:S(2)}, u32[]{:S(2)}) collective-permute-start(bf16[64,1024]{1,0:T(8,128)(2,1)S(1)} %collective-permute-done.13), channel_id=1, source_target_pairs={{1,0},{2,1},{3,2},{4,3},{5,4},{6,5},{7,6},{8,7},{9,8},{10,9},{11,1... | collective-permute-start | bytes 393224 | tf_op jit(solution)/shard_map/ppermute | solution.py:27
  101.4 85.5 %while.15 = (s32[]{:T(128)}, f32[1024,4,2]{0,2,1:T(2,128)S(1)}, f32[1024,4,2]{0,2,1:T(2,128)S(1)}, f32[1024,4,2,128]{0,3,2,1:T(8,128)}, s32[4,512]{1,0:T(4,128)S...) while((s32[]{:T(128)}, f32[1024,4,2]{0,2,1:T(2,128)S(1)}, ...), condition=%wide.region_12.13_spmd.clone, body=%wide.region_9.12_spmd.clone.sunk | while | flops 2206780416 | bytes 69814488 | solution.py:201
  105.9 4.3 %fusion.139 = (f32[1024,4,2]{0,2,1:T(2,128)S(1)}, f32[4,512,1024,2]{2,1,3,0:T(8,128)S(1)}) fusion(pred[1024,512]{0,1:T(8,128)(4,1)S(1)} %compare_or_fusion.2, bf16[1024,4,2,128]{3,0,2,1:T(8,128)(2,1)S(1)} %get-tuple-element.291, bf16[1,512,4,128]{3,2,1,0:T(4,128)(2,1)} %get-tuple-element.256), kind=kOutput, calls=%fused_computation.4.clone.1 | convolution fusion | flops 1086316544 | bytes 19955712 | tf_op jit(solution)/shard_map/while/body/eval_jaxpr/nkgd,pkd->nkgp/dot_general | solution.py:176
  110.3 4.1 %fusion.141 = f32[1024,4,2]{0,2,1:T(2,128)S(1)} fusion(f32[4,512,1024,2]{2,1,3,0:T(8,128)S(1)} %get-tuple-element.258, f32[1024,4,2]{0,2,1:T(2,128)S(1)} %fusion.140, pred[1024,512]{0,1:T(8,128)(4,1)S(1)} %compare_or_fusion.2), kind=kLoop, calls=%fused_computation.6.clone.1 | loop fusion | flops 20963328 | bytes 17367040 | tf_op jit(solution)/shard_map/while/body/eval_jaxpr/reduce_sum | solution.py:187
  114.5 7.1 %bitcast_add_fusion.2 = f32[1024,4,2,128]{0,3,2,1:T(8,128)} fusion(f32[1024,4,2,128]{0,3,2,1:T(8,128)} %get-tuple-element.276, f32[4,512,1024,2]{2,1,3,0:T(8,128)S(1)} %get-tuple-element.258, f32[1024,4,2]{0,2,1:T(2,128)S(1)} %fusion.140, pred[1024,512]{0,1:T(8,128)(4,1)S(1)} %compare_or_fusion.2, f32[1024,4,2]{0,2,1:T(2,128)S(1)} %get-tuple-element.260, ...), kind=kOutput, calls=%fused_computation.9.clone.1 | convolution fusion | flops 1097859072 | bytes 26279936 | tf_op jit(solution)/shard_map/while/body/eval_jaxpr/nkgp,pkd->nkgd/dot_general | solution.py:188
  126.2 4.3 %fusion.139 = (f32[1024,4,2]{0,2,1:T(2,128)S(1)}, f32[4,512,1024,2]{2,1,3,0:T(8,128)S(1)}) fusion(pred[1024,512]{0,1:T(8,128)(4,1)S(1)} %compare_or_fusion.2, bf16[1024,4,2,128]{3,0,2,1:T(8,128)(2,1)S(1)} %get-tuple-element.291, bf16[1,512,4,128]{3,2,1,0:T(4,128)(2,1)} %get-tuple-element.256), kind=kOutput, calls=%fused_computation.4.clone.1 | convolution fusion | flops 1086316544 | bytes 19955712 | tf_op jit(solution)/shard_map/while/body/eval_jaxpr/nkgd,pkd->nkgp/dot_general | solution.py:176
  134.7 8.7 %bitcast_add_fusion.2 = f32[1024,4,2,128]{0,3,2,1:T(8,128)} fusion(f32[1024,4,2,128]{0,3,2,1:T(8,128)} %get-tuple-element.276, f32[4,512,1024,2]{2,1,3,0:T(8,128)S(1)} %get-tuple-element.258, f32[1024,4,2]{0,2,1:T(2,128)S(1)} %fusion.140, pred[1024,512]{0,1:T(8,128)(4,1)S(1)} %compare_or_fusion.2, f32[1024,4,2]{0,2,1:T(2,128)S(1)} %get-tuple-element.260, ...), kind=kOutput, calls=%fused_computation.9.clone.1 | convolution fusion | flops 1097859072 | bytes 26279936 | tf_op jit(solution)/shard_map/while/body/eval_jaxpr/nkgp,pkd->nkgd/dot_general | solution.py:188
  147.9 4.3 %fusion.139 = (f32[1024,4,2]{0,2,1:T(2,128)S(1)}, f32[4,512,1024,2]{2,1,3,0:T(8,128)S(1)}) fusion(pred[1024,512]{0,1:T(8,128)(4,1)S(1)} %compare_or_fusion.2, bf16[1024,4,2,128]{3,0,2,1:T(8,128)(2,1)S(1)} %get-tuple-element.291, bf16[1,512,4,128]{3,2,1,0:T(4,128)(2,1)} %get-tuple-element.256), kind=kOutput, calls=%fused_computation.4.clone.1 | convolution fusion | flops 1086316544 | bytes 19955712 | tf_op jit(solution)/shard_map/while/body/eval_jaxpr/nkgd,pkd->nkgp/dot_general | solution.py:176
  156.5 8.7 %bitcast_add_fusion.2 = f32[1024,4,2,128]{0,3,2,1:T(8,128)} fusion(f32[1024,4,2,128]{0,3,2,1:T(8,128)} %get-tuple-element.276, f32[4,512,1024,2]{2,1,3,0:T(8,128)S(1)} %get-tuple-element.258, f32[1024,4,2]{0,2,1:T(2,128)S(1)} %fusion.140, pred[1024,512]{0,1:T(8,128)(4,1)S(1)} %compare_or_fusion.2, f32[1024,4,2]{0,2,1:T(2,128)S(1)} %get-tuple-element.260, ...), kind=kOutput, calls=%fused_computation.9.clone.1 | convolution fusion | flops 1097859072 | bytes 26279936 | tf_op jit(solution)/shard_map/while/body/eval_jaxpr/nkgp,pkd->nkgd/dot_general | solution.py:188
  169.7 4.3 %fusion.139 = (f32[1024,4,2]{0,2,1:T(2,128)S(1)}, f32[4,512,1024,2]{2,1,3,0:T(8,128)S(1)}) fusion(pred[1024,512]{0,1:T(8,128)(4,1)S(1)} %compare_or_fusion.2, bf16[1024,4,2,128]{3,0,2,1:T(8,128)(2,1)S(1)} %get-tuple-element.291, bf16[1,512,4,128]{3,2,1,0:T(4,128)(2,1)} %get-tuple-element.256), kind=kOutput, calls=%fused_computation.4.clone.1 | convolution fusion | flops 1086316544 | bytes 19955712 | tf_op jit(solution)/shard_map/while/body/eval_jaxpr/nkgd,pkd->nkgp/dot_general | solution.py:176
  178.2 8.7 %bitcast_add_fusion.2 = f32[1024,4,2,128]{0,3,2,1:T(8,128)} fusion(f32[1024,4,2,128]{0,3,2,1:T(8,128)} %get-tuple-element.276, f32[4,512,1024,2]{2,1,3,0:T(8,128)S(1)} %get-tuple-element.258, f32[1024,4,2]{0,2,1:T(2,128)S(1)} %fusion.140, pred[1024,512]{0,1:T(8,128)(4,1)S(1)} %compare_or_fusion.2, f32[1024,4,2]{0,2,1:T(2,128)S(1)} %get-tuple-element.260, ...), kind=kOutput, calls=%fused_computation.9.clone.1 | convolution fusion | flops 1097859072 | bytes 26279936 | tf_op jit(solution)/shard_map/while/body/eval_jaxpr/nkgp,pkd->nkgd/dot_general | solution.py:188
  187.0 5.4 %copy.208 = f32[1024,1024]{1,0:T(8,128)} copy(f32[1024,1024]{0,1:T(8,128)} %bitcast.206) | data formatting | bytes 8388608 | tf_op jit(solution)/shard_map/reshape;reshape | solution.py:209
  192.4 57.6 %pmax.7 = bf16[1024,8]{0,1:T(8,128)(2,1)S(1)} all-reduce(bf16[1024,8]{0,1:T(8,128)(2,1)S(1)} %convert_element_type.114), channel_id=1, replica_groups=mesh['kv'=2,'seq'=16] {'seq'}, use_global_device_ids=true, to_apply=%region_13.14 | all-reduce | flops 8192 | bytes 32768 | tf_op jit(solution)/shard_map/pmax | solution.py:207
  262.1 41.7 %reduce-scatter.10.cloned.1.call-done = bf16[64,8]{1,0:T(8,128)(2,1)} async-done(((bf16[1024,8]{1,0:T(8,128)(2,1)}), bf16[64,8]{1,0:T(8,128)(2,1)}) %reduce-scatter.10.cloned.1.call-update) | async-done | bytes 1040
  304.9 63.3 %reduce-scatter.6.cloned.1.call-done = bf16[64,1024]{1,0:T(8,128)(2,1)} async-done(((bf16[1024,1024]{1,0:T(8,128)(2,1)}), bf16[64,1024]{1,0:T(8,128)(2,1)}) %reduce-scatter.6.cloned.1.call-update) | async-done | bytes 131088 | tf_op jit(solution)/shard_map/reduce_scatter | solution.py:213
  373.8 9.8 %reduce-scatter.8.cloned.1.call-done = bf16[64,1024]{1,0:T(8,128)(2,1)} async-done(((bf16[64,2048]{1,0:T(8,128)(2,1)}), bf16[64,1024]{1,0:T(8,128)(2,1)}) %reduce-scatter.8.cloned.1.call-update) | async-done | bytes 131088 | tf_op jit(solution)/shard_map/reduce_scatter | solution.py:236
  (285 shorter events, 97.8 us)
Async XLA Ops:
  7.2 19.7 %copy-start = (bf16[2048,512]{1,0:T(8,128)(2,1)S(1)}, bf16[2048,512]{1,0:T(8,128)(2,1)}, u32[]{:S(2)}) copy-start(bf16[2048,512]{1,0:T(8,128)(2,1)} %param.21) | copy-start | bytes 6291460
  7.2 296.6 %reduce-scatter.10.cloned.1.call-start = ((), (), s32[]{:S(2)}) async-start(), calls=%async_computation.5 | async-start | bytes 278528
  7.2 14.2 %copy-start.29 = (f32[64]{0:T(128)}, f32[64]{0:T(128)S(1)}, u32[]{:S(2)}) copy-start(f32[64]{0:T(128)S(1)} %multiply_exponential_fusion) | copy-start | bytes 772
  15.4 12.0 %copy-start.4 = (bf16[64,2048]{1,0:T(8,128)(2,1)}, bf16[64,2048]{1,0:T(8,128)(2,1)S(1)}, u32[]{:S(2)}) copy-start(bf16[64,2048]{1,0:T(8,128)(2,1)S(1)} %all_gather.3) | copy-start | bytes 786436
  23.2 17.8 %collective-permute-start.8 = (bf16[64,1024]{1,0:T(8,128)(2,1)S(1)}, bf16[64,1024]{1,0:T(8,128)(2,1)S(1)}, u32[]{:S(2)}, u32[]{:S(2)}) collective-permute-start(bf16[64,1024]{1,0:T(8,128)(2,1)S(1)} %fusion.35), channel_id=1, source_target_pairs={{1,0},{2,1},{3,2},{4,3},{5,4},{6,5},{7,6},{8,7},{9,8},{10,9},{11,1... | collective-permute-start | bytes 393224 | tf_op jit(solution)/shard_map/ppermute | solution.py:27
  26.5 7.1 %collective-permute-start = (bf16[64,1024]{1,0:T(8,128)(2,1)S(1)}, bf16[64,1024]{1,0:T(8,128)(2,1)S(1)}, u32[]{:S(2)}, u32[]{:S(2)}) collective-permute-start(bf16[64,1024]{1,0:T(8,128)(2,1)S(1)} %fusion.35), channel_id=1, source_target_pairs={{0,1},{1,2},{2,3},{3,4},{4,5},{5,6},{6,7},{7,8},{8,9},{9,10},{10,1... | collective-permute-start | bytes 393224 | tf_op jit(solution)/shard_map/ppermute | solution.py:25
  27.5 64.4 %copy-start.6 = (f32[64,512]{1,0:T(8,128)}, f32[64,512]{1,0:T(8,128)S(1)}, u32[]{:S(2)}) copy-start(f32[64,512]{1,0:T(8,128)S(1)} %fusion.96) | copy-start | bytes 393220
  33.6 7.2 %collective-permute-start.1 = (bf16[64,1024]{1,0:T(8,128)(2,1)S(1)}, bf16[64,1024]{1,0:T(8,128)(2,1)S(1)}, u32[]{:S(2)}, u32[]{:S(2)}) collective-permute-start(bf16[64,1024]{1,0:T(8,128)(2,1)S(1)} %collective-permute-done), channel_id=1, source_target_pairs={{0,1},{1,2},{2,3},{3,4},{4,5},{5,6},{6,7},{7,8},{8,9},{9,10},{10,1... | collective-permute-start | bytes 393224 | tf_op jit(solution)/shard_map/ppermute | solution.py:25
  40.8 7.2 %collective-permute-start.2 = (bf16[64,1024]{1,0:T(8,128)(2,1)S(1)}, bf16[64,1024]{1,0:T(8,128)(2,1)S(1)}, u32[]{:S(2)}, u32[]{:S(2)}) collective-permute-start(bf16[64,1024]{1,0:T(8,128)(2,1)S(1)} %collective-permute-done.1), channel_id=1, source_target_pairs={{0,1},{1,2},{2,3},{3,4},{4,5},{5,6},{6,7},{7,8},{8,9},{9,10},{10,1... | collective-permute-start | bytes 393224 | tf_op jit(solution)/shard_map/ppermute | solution.py:25
  40.9 7.2 %collective-permute-start.9 = (bf16[64,1024]{1,0:T(8,128)(2,1)S(1)}, bf16[64,1024]{1,0:T(8,128)(2,1)S(1)}, u32[]{:S(2)}, u32[]{:S(2)}) collective-permute-start(bf16[64,1024]{1,0:T(8,128)(2,1)S(1)} %collective-permute-done.8), channel_id=1, source_target_pairs={{1,0},{2,1},{3,2},{4,3},{5,4},{6,5},{7,6},{8,7},{9,8},{10,9},{11,1... | collective-permute-start | bytes 393224 | tf_op jit(solution)/shard_map/ppermute | solution.py:27
  48.0 7.2 %collective-permute-start.3 = (bf16[64,1024]{1,0:T(8,128)(2,1)S(1)}, bf16[64,1024]{1,0:T(8,128)(2,1)S(1)}, u32[]{:S(2)}, u32[]{:S(2)}) collective-permute-start(bf16[64,1024]{1,0:T(8,128)(2,1)S(1)} %collective-permute-done.2), channel_id=1, source_target_pairs={{0,1},{1,2},{2,3},{3,4},{4,5},{5,6},{6,7},{7,8},{8,9},{9,10},{10,1... | collective-permute-start | bytes 393224 | tf_op jit(solution)/shard_map/ppermute | solution.py:25
  48.2 7.1 %collective-permute-start.10 = (bf16[64,1024]{1,0:T(8,128)(2,1)S(1)}, bf16[64,1024]{1,0:T(8,128)(2,1)S(1)}, u32[]{:S(2)}, u32[]{:S(2)}) collective-permute-start(bf16[64,1024]{1,0:T(8,128)(2,1)S(1)} %collective-permute-done.9), channel_id=1, source_target_pairs={{1,0},{2,1},{3,2},{4,3},{5,4},{6,5},{7,6},{8,7},{9,8},{10,9},{11,1... | collective-permute-start | bytes 393224 | tf_op jit(solution)/shard_map/ppermute | solution.py:27
  55.2 7.2 %collective-permute-start.4 = (bf16[64,1024]{1,0:T(8,128)(2,1)S(1)}, bf16[64,1024]{1,0:T(8,128)(2,1)S(1)}, u32[]{:S(2)}, u32[]{:S(2)}) collective-permute-start(bf16[64,1024]{1,0:T(8,128)(2,1)S(1)} %collective-permute-done.3), channel_id=1, source_target_pairs={{0,1},{1,2},{2,3},{3,4},{4,5},{5,6},{6,7},{7,8},{8,9},{9,10},{10,1... | collective-permute-start | bytes 393224 | tf_op jit(solution)/shard_map/ppermute | solution.py:25
  55.2 7.3 %collective-permute-start.11 = (bf16[64,1024]{1,0:T(8,128)(2,1)S(1)}, bf16[64,1024]{1,0:T(8,128)(2,1)S(1)}, u32[]{:S(2)}, u32[]{:S(2)}) collective-permute-start(bf16[64,1024]{1,0:T(8,128)(2,1)S(1)} %collective-permute-done.10), channel_id=1, source_target_pairs={{1,0},{2,1},{3,2},{4,3},{5,4},{6,5},{7,6},{8,7},{9,8},{10,9},{11,1... | collective-permute-start | bytes 393224 | tf_op jit(solution)/shard_map/ppermute | solution.py:27
  62.4 7.2 %collective-permute-start.5 = (bf16[64,1024]{1,0:T(8,128)(2,1)S(1)}, bf16[64,1024]{1,0:T(8,128)(2,1)S(1)}, u32[]{:S(2)}, u32[]{:S(2)}) collective-permute-start(bf16[64,1024]{1,0:T(8,128)(2,1)S(1)} %collective-permute-done.4), channel_id=1, source_target_pairs={{0,1},{1,2},{2,3},{3,4},{4,5},{5,6},{6,7},{7,8},{8,9},{9,10},{10,1... | collective-permute-start | bytes 393224 | tf_op jit(solution)/shard_map/ppermute | solution.py:25
  62.5 7.3 %collective-permute-start.12 = (bf16[64,1024]{1,0:T(8,128)(2,1)S(1)}, bf16[64,1024]{1,0:T(8,128)(2,1)S(1)}, u32[]{:S(2)}, u32[]{:S(2)}) collective-permute-start(bf16[64,1024]{1,0:T(8,128)(2,1)S(1)} %collective-permute-done.11), channel_id=1, source_target_pairs={{1,0},{2,1},{3,2},{4,3},{5,4},{6,5},{7,6},{8,7},{9,8},{10,9},{11,1... | collective-permute-start | bytes 393224 | tf_op jit(solution)/shard_map/ppermute | solution.py:27
  69.6 7.2 %collective-permute-start.6 = (bf16[64,1024]{1,0:T(8,128)(2,1)S(1)}, bf16[64,1024]{1,0:T(8,128)(2,1)S(1)}, u32[]{:S(2)}, u32[]{:S(2)}) collective-permute-start(bf16[64,1024]{1,0:T(8,128)(2,1)S(1)} %collective-permute-done.5), channel_id=1, source_target_pairs={{0,1},{1,2},{2,3},{3,4},{4,5},{5,6},{6,7},{7,8},{8,9},{9,10},{10,1... | collective-permute-start | bytes 393224 | tf_op jit(solution)/shard_map/ppermute | solution.py:25
  69.8 7.7 %collective-permute-start.13 = (bf16[64,1024]{1,0:T(8,128)(2,1)S(1)}, bf16[64,1024]{1,0:T(8,128)(2,1)S(1)}, u32[]{:S(2)}, u32[]{:S(2)}) collective-permute-start(bf16[64,1024]{1,0:T(8,128)(2,1)S(1)} %collective-permute-done.12), channel_id=1, source_target_pairs={{1,0},{2,1},{3,2},{4,3},{5,4},{6,5},{7,6},{8,7},{9,8},{10,9},{11,1... | collective-permute-start | bytes 393224 | tf_op jit(solution)/shard_map/ppermute | solution.py:27
  76.8 7.1 %collective-permute-start.7 = (bf16[64,1024]{1,0:T(8,128)(2,1)S(1)}, bf16[64,1024]{1,0:T(8,128)(2,1)S(1)}, u32[]{:S(2)}, u32[]{:S(2)}) collective-permute-start(bf16[64,1024]{1,0:T(8,128)(2,1)S(1)} %collective-permute-done.6), channel_id=1, source_target_pairs={{0,1},{1,2},{2,3},{3,4},{4,5},{5,6},{6,7},{7,8},{8,9},{9,10},{10,1... | collective-permute-start | bytes 393224 | tf_op jit(solution)/shard_map/ppermute | solution.py:25
  77.5 16.4 %collective-permute-start.14 = (bf16[64,1024]{1,0:T(8,128)(2,1)S(1)}, bf16[64,1024]{1,0:T(8,128)(2,1)S(1)}, u32[]{:S(2)}, u32[]{:S(2)}) collective-permute-start(bf16[64,1024]{1,0:T(8,128)(2,1)S(1)} %collective-permute-done.13), channel_id=1, source_target_pairs={{1,0},{2,1},{3,2},{4,3},{5,4},{6,5},{7,6},{8,7},{9,8},{10,9},{11,1... | collective-permute-start | bytes 393224 | tf_op jit(solution)/shard_map/ppermute | solution.py:27
  251.0 117.2 %reduce-scatter.6.cloned.1.call-start = ((), (), s32[]{:S(2)}) async-start(), calls=%async_computation.3 | async-start | bytes 2228224 | tf_op jit(solution)/shard_map/reduce_scatter | solution.py:213
  255.6 127.9 %reduce-scatter.8.cloned.1.call-start = ((), (), s32[]{:S(2)}) async-start(), calls=%async_computation.4 | async-start | bytes 393216 | tf_op jit(solution)/shard_map/reduce_scatter | solution.py:236
  368.7 16.5 %copy-start.1 = (bf16[2048,512]{1,0:T(8,128)(2,1)S(1)}, bf16[2048,512]{1,0:T(8,128)(2,1)}, u32[]{:S(2)}) copy-start(bf16[2048,512]{1,0:T(8,128)(2,1)} %param.21) | copy-start | bytes 6291460
  368.7 14.9 %copy-start.12 = (bf16[64,1024]{1,0:T(8,128)(2,1)S(1)}, bf16[64,1024]{1,0:T(8,128)(2,1)}, u32[]{:S(2)}) copy-start(bf16[64,1024]{1,0:T(8,128)(2,1)} %param.18) | copy-start | bytes 393220
  (40 other events, 143.6 us)
Sparse Core Ops, SparseCore 0:
  251.1 52.6 reduce-scatter.9
  307.5 60.6 reduce-scatter.5
  372.9 10.6 reduce-scatter.7
